TPU v7x, 32 devices: a whole 2x2x4 slice. The times are simulated.
32 devices in a mesh: dom: 4 (over z), row: 4 (over y, x), col: 2 (over core).
Axes of the slice: x: 2, y: 2, z: 4, core: 2. Of those that a mesh axis runs over, the one named last changes fastest.
Arguments:
- currents: bfloat16 [4, 64, 4096], P('dom', None, ('col', 'row')), may hold values from -6 to 6
- shared_basis: bfloat16 [4, 64, 4096], P('dom', None, 'col'), may hold values from -0.25 to 0.25
- self_v: bfloat16 [4, 8, 8, 64, 512], P('dom', 'row', 'col'), may hold values from -0.25 to 0.25
- self_u: bfloat16 [4, 8, 8, 64, 512], P('dom', 'row', 'col'), may hold values from -0.25 to 0.25
- self_rank: int32 [4, 8, 8], P('dom', 'row', 'col'), may hold values from 16 to 64
- coupling_u: bfloat16 [4, 8, 4, 4, 64, 512], P('dom', 'row', None, 'col'), may hold values from -0.1875 to 0.1875
- coupling_rank: int32 [4, 8, 4, 4], P('dom', 'row', None, 'col'), may hold values from 16 to 64
- link_tiles: int32 [4, 8, 4, 4], P('dom', 'row', None, 'col'), may hold values from 0 to 3
- incident: float32 [4, 64, 4096], P('dom', 'col', 'row'), may hold values from -6 to 6
Outputs:
- residual: float32 [4, 64, 4096], P('dom', 'col', 'row')
Inputs may be any that keep to these rules, and one draw needn't show every extreme that they name: `link_tiles`: entries may repeat within a list.
All inputs are finite; a program needn't handle non-finite values.
Results may differ from a plain program's by a relative error of at most 0.0022.
Values may be sent and summed in bfloat16 or wider, within the bound.
A program may use at most 64 MiB of HBM per device.

v0:
```python
import jax
import jax.numpy as jnp
from jax import lax
from jax.sharding import PartitionSpec as P


def shards(
    currents,
    shared_basis,
    self_v,
    self_u,
    self_rank,
    coupling_u,
    coupling_rank,
    link_tiles,
    incident,
):
    col_count = lax.axis_size("col")
    row_count = lax.axis_size("row")
    dom_count = lax.axis_size("dom")
    angles = currents.shape[1]
    tile_len = self_v.shape[-1]
    rank_len = self_v.shape[-2]
    own_tiles = currents.shape[2] // tile_len
    block_tiles = own_tiles * row_count
    window_rows = self_v.shape[1]
    link_count = link_tiles.shape[-1]
    gathered = lax.all_gather(currents, "row", axis=2, tiled=True)
    current_tiles = gathered[0].reshape(angles, block_tiles, tile_len)
    levels = jnp.arange(rank_len, dtype=jnp.int32)
    keep_self = (levels[None, None, :] < self_rank[0][:, :, None]).astype(jnp.float32)
    selfproj = jnp.einsum(
        "tjkn,ajn->tjka", self_v[0], current_tiles, preferred_element_type=jnp.float32
    )
    selfproj = (selfproj * keep_self[..., None]).astype(jnp.bfloat16)
    bases = shared_basis[0].reshape(rank_len, block_tiles, tile_len)
    projections = jnp.einsum(
        "kjn,ajn->jka", bases, current_tiles, preferred_element_type=jnp.float32
    ).astype(jnp.bfloat16)
    flat_proj = lax.all_gather(projections, "dom", axis=0, tiled=True)
    picks = jnp.arange(dom_count, dtype=jnp.int32)[None, :, None] * block_tiles + link_tiles[0]
    chosen = jnp.take(flat_proj, picks.reshape(-1), axis=0)
    chosen = chosen.reshape(window_rows, dom_count, link_count, rank_len, angles)
    keep_cpl = (levels < coupling_rank[0][..., None]).astype(jnp.bfloat16)
    chosen = chosen * keep_cpl[..., None]
    field_self = jnp.einsum(
        "tjkn,tjka->atn", self_u[0], selfproj, preferred_element_type=jnp.float32
    )
    field_cpl = jnp.einsum(
        "temkn,temka->atn", coupling_u[0], chosen, preferred_element_type=jnp.float32
    )
    summed = lax.psum_scatter(
        (field_self + field_cpl).reshape(
            lax.axis_size("col") * (angles // col_count), window_rows * tile_len
        ),
        "col",
        scatter_dimension=0,
        tiled=True,
    )
    return (incident[0] - summed)[None]


def solution(mesh):
    return jax.shard_map(
        shards,
        mesh=mesh,
        in_specs=(
            P("dom", None, ("col", "row")),
            P("dom", None, "col"),
            P("dom", "row", "col", None, None),
            P("dom", "row", "col", None, None),
            P("dom", "row", "col"),
            P("dom", "row", None, "col", None, None),
            P("dom", "row", None, "col"),
            P("dom", "row", None, "col"),
            P("dom", "col", "row"),
        ),
        out_specs=P("dom", "col", "row"),
        check_vma=False,
    )
```

profile of v0, /device:TPU:0, one launch (start us, length us, event | category | flops | bytes accessed | tf_op | source)
XLA Modules:
  0.0 54.6 jit_solution(8625819946076858705)
XLA Ops:
  6.5 0.0 copy-start
  6.5 0.0 reduce-scatter.2.cloned.1.call-start
  6.5 10.9 %all_gather.6 = bf16[1,64,2048]{2,1,0:T(8,128)(2,1)S(1)} all-gather(bf16[1,64,512]{2,1,0:T(8,128)(2,1)} %param.9), channel_id=1, replica_groups=mesh['dom'=4,'row'=4,'col'=2] {'row'}, dimensions={2}, use_global_device_ids=true | all-gather | bytes 327680 | tf_op jit(solution)/shard_map/all_gather | solution.py:28
  17.4 0.0 copy-start.3
  17.4 0.2 reshape_squeeze.6
  17.6 0.8 %copy-done.3 = bf16[1,64,2048]{2,1,0:T(8,128)(2,1)S(1)} copy-done((bf16[1,64,2048]{2,1,0:T(8,128)(2,1)S(1)}, bf16[1,64,2048]{2,1,0:T(8,128)(2,1)}, u32[]{:S(2)}) %copy-start.3) | copy-done | bytes 262168
  18.4 0.2 reshape_squeeze.7
  18.6 0.2 convolution_convert_fusion
  18.8 0.0 copy-start.5
  18.8 14.4 %all_gather.7 = bf16[16,64,64]{2,1,0:T(8,128)(2,1)S(1)} all-gather(bf16[4,64,64]{2,1,0:T(8,128)(2,1)S(1)} %convolution_convert_fusion), channel_id=1, replica_groups=mesh['dom'=4,'row'=4,'col'=2] {'dom'}, dimensions={0}, use_global_device_ids=true | all-gather | bytes 163840 | tf_op jit(solution)/shard_map/all_gather | solution.py:40
  33.2 0.0 copy-done.5
  33.2 0.1 copy.29
  33.3 0.1 add.49.clone
  33.4 0.1 add.52
  33.5 0.1 squeeze.21
  33.6 0.6 %gather_fusion = bf16[16,64,64]{2,1,0:T(8,128)(2,1)S(1)} fusion(bf16[16,64,64]{2,1,0:T(8,128)(2,1)S(1)} %all_gather.7, s32[1024]{0:T(1024)S(1)} %pad_clamp_fusion), kind=kCustom, calls=%fused_computation | custom fusion | bytes 262208 | tf_op jit(solution)/shard_map/jit(_take)/gather | solution.py:42
  34.2 0.2 copy.30
  34.4 0.0 copy-start.6
  34.4 0.1 copy.25
  34.5 0.5 %copy-done.6 = s32[1,2,4,2]{2,3,1,0:T(2,128)S(1)} copy-done((s32[1,2,4,2]{2,3,1,0:T(2,128)S(1)}, s32[1,2,4,2]{2,3,1,0:T(2,128)}, u32[]{:S(2)}) %copy-start.6) | copy-done | bytes 88
  35.0 0.1 copy.31
  35.1 0.1 compare_convert_fusion
  35.2 0.0 copy-start.7
  35.2 0.7 %copy-done.7 = s32[1,2,4]{2,1,0:T(2,128)S(1)} copy-done((s32[1,2,4]{2,1,0:T(2,128)S(1)}, s32[1,2,4]{2,1,0:T(2,128)}, u32[]{:S(2)}) %copy-start.7) | copy-done | bytes 56
  35.9 0.1 fusion.21
  36.0 0.0 copy-done
  36.0 0.0 copy-start.1
  36.0 0.0 copy-start.2
  36.0 0.4 convolution_bitcast_fusion.2
  36.4 0.6 %copy-done.1 = bf16[1,2,4,64,512]{4,3,2,1,0:T(8,128)(2,1)S(1)} copy-done((bf16[1,2,4,64,512]{4,3,2,1,0:T(8,128)(2,1)S(1)}, bf16[1,2,4,64,512]{4,3,2,1,0:T(8,128)(2,1)}, u32[]{:S(2)}) %copy-start.1) | copy-done | bytes 524312
  37.0 0.2 copy-done.2
  37.2 0.6 %fusion.2 = f32[2,8,8,512]{3,2,1,0:T(8,128)S(1)} fusion(f32[2,64,512]{2,1,0:T(8,128)S(1)} %convolution_bitcast_fusion.2, bf16[1,2,4,64,512]{4,3,2,1,0:T(8,128)(2,1)S(1)} %copy-done.1, bf16[1,2,4,64,512]{4,3,2,1,0:T(8,128)(2,1)S(1)} %copy-done.2, bf16[64,4,512]{2,1,0:T(4,128)(2,1)S(1)} %reshape_squeeze.6, f32[2,4,64]{2,1,0:T(4,128)S(1)} %fusion.21), kind=kOutput, calls=%fused_computation.6 | convolution fusion | flops 67239936 | bytes 1837056 | tf_op jit(solution)/shard_map/tjkn,tjka->atn/dot_general | solution.py:46
  37.8 0.7 %copy.36 = f32[2,8,8,512]{3,2,0,1:T(8,128)} copy(f32[2,8,8,512]{3,2,1,0:T(8,128)S(1)} %fusion.2) | data formatting | bytes 524288 | tf_op jit(solution)/shard_map/reshape | solution.py:53
  38.5 0.0 copy-start.4
  38.5 0.0 reduce-scatter.2.cloned.1.call-update
  38.5 7.6 %reduce-scatter.2.cloned.1.call-done = f32[32,1024]{1,0:T(8,128)} async-done(((f32[64,1024]{1,0:T(8,128)}), f32[32,1024]{1,0:T(8,128)}) %reduce-scatter.2.cloned.1.call-update) | async-done | bytes 131088 | tf_op jit(solution)/shard_map/reduce_scatter | solution.py:52
  46.2 0.0 copy-done.4
  46.2 1.6 %fusion.17 = f32[1,32,1024]{2,1,0:T(8,128)} fusion(f32[32,1024]{1,0:T(8,128)} %reduce-scatter.2.cloned.1.call-done, f32[1,32,1024]{2,1,0:T(8,128)S(1)} %copy-done.4), kind=kLoop, calls=%fused_computation.20 | loop fusion | flops 32768 | bytes 393216 | tf_op jit(solution)/shard_map/broadcast_in_dim | solution.py:60
  (4 shorter events, 0.0 us)
Async XLA Ops:
  6.5 29.4 %copy-start = (bf16[1,2,4,2,64,512]{5,4,3,2,1,0:T(8,128)(2,1)S(1)}, bf16[1,2,4,2,64,512]{5,4,3,2,1,0:T(8,128)(2,1)}, u32[]{:S(2)}) copy-start(bf16[1,2,4,2,64,512]{5,4,3,2,1,0:T(8,128)(2,1)} %param.14) | copy-start | bytes 3145732
  6.5 39.6 %reduce-scatter.2.cloned.1.call-start = ((), (), s32[]{:S(2)}) async-start(), calls=%async_computation.1 | async-start | bytes 393216 | tf_op jit(solution)/shard_map/reduce_scatter | solution.py:52
  17.4 1.0 %copy-start.3 = (bf16[1,64,2048]{2,1,0:T(8,128)(2,1)S(1)}, bf16[1,64,2048]{2,1,0:T(8,128)(2,1)}, u32[]{:S(2)}) copy-start(bf16[1,64,2048]{2,1,0:T(8,128)(2,1)} %param.10) | copy-start | bytes 786436
  18.8 14.4 %copy-start.5 = (s32[1,2,4,2]{2,3,1,0:T(2,128)S(1)}, s32[1,2,4,2]{2,3,1,0:T(2,128)}, u32[]{:S(2)}) copy-start(s32[1,2,4,2]{2,3,1,0:T(2,128)} %param.16) | copy-start | bytes 196
  34.4 0.7 %copy-start.6 = (s32[1,2,4,2]{2,3,1,0:T(2,128)S(1)}, s32[1,2,4,2]{2,3,1,0:T(2,128)}, u32[]{:S(2)}) copy-start(s32[1,2,4,2]{2,3,1,0:T(2,128)} %param.15) | copy-start | bytes 196
  35.2 0.7 %copy-start.7 = (s32[1,2,4]{2,1,0:T(2,128)S(1)}, s32[1,2,4]{2,1,0:T(2,128)}, u32[]{:S(2)}) copy-start(s32[1,2,4]{2,1,0:T(2,128)} %param.13) | copy-start | bytes 100
  36.0 1.0 %copy-start.1 = (bf16[1,2,4,64,512]{4,3,2,1,0:T(8,128)(2,1)S(1)}, bf16[1,2,4,64,512]{4,3,2,1,0:T(8,128)(2,1)}, u32[]{:S(2)}) copy-start(bf16[1,2,4,64,512]{4,3,2,1,0:T(8,128)(2,1)} %param.12) | copy-start | bytes 1572868
  36.0 1.2 %copy-start.2 = (bf16[1,2,4,64,512]{4,3,2,1,0:T(8,128)(2,1)S(1)}, bf16[1,2,4,64,512]{4,3,2,1,0:T(8,128)(2,1)}, u32[]{:S(2)}) copy-start(bf16[1,2,4,64,512]{4,3,2,1,0:T(8,128)(2,1)} %param.11) | copy-start | bytes 1572868
  38.5 7.7 %copy-start.4 = (f32[1,32,1024]{2,1,0:T(8,128)S(1)}, f32[1,32,1024]{2,1,0:T(8,128)}, u32[]{:S(2)}) copy-start(f32[1,32,1024]{2,1,0:T(8,128)} %param.17) | copy-start | bytes 393220
Sparse Core Ops, SparseCore 0:
  38.6 7.4 reduce-scatter.1
where the time goes:
time: 54.9 us; the launch traced here: 54.6 us
  blocking collectives  25.3 us (46%)
  between operations  13.5 us (25%)
  waiting for transfers between devices  7.66 us (14%)
  local copies, waits for them, and re-layouts  5.2 us (9%)
  other arithmetic  1.75 us (3%)
  matrix products  1.23 us (2%)
    all_gather x1, blocking collectives, shards(): flat_proj = lax.all_gather(projections, 'dom', axis=0, tiled=True)  14.4 us
    all_gather x1, blocking collectives, shards(): gathered = lax.all_gather(currents, 'row', axis=2, tiled=True)  10.9 us
    reduce_scatter x1, waiting for transfers between devices, shards(): lax.psum_scatter((field_self + field_cpl).reshape(lax.axis_size('col') *...  7.64 us
    unnamed x17, local copies, waits for them, and re-layouts  2.88 us
    broadcast_in_dim x1, other arithmetic, shards(): return (incident[0] - summed)[None]  1.57 us
  transfers between devices with their start and end apart: 1, of which 1 were waited for; matrix products, arithmetic and copies ran while one was open for 0% of the time, Pallas kernels for 0%

commit v1 on v0

v1 whole, which is shorter than its diff:
```python
import functools

import jax
import jax.numpy as jnp
from jax import lax
from jax.experimental import pallas as pl
from jax.experimental.pallas import tpu as pltpu
from jax.sharding import PartitionSpec as P

MESH = pl.DeviceIdType.MESH
LANES = 128
NT = (((1,), (1,)), ((), ()))


def kernel(
    sizes,
    self_rank,
    coupling_rank,
    link_tiles,
    currents,
    basis,
    self_v,
    self_u,
    coupling_u,
    out,
    cur_all,
    basis_own,
    v_buf,
    u_buf,
    cu_buf,
    proj,
    acc,
    part,
    landed,
    in_sem,
    cur_send,
    cur_recv,
    dom_send,
    dom_recv,
    row_send,
    row_recv,
    col_send,
    col_recv,
):
    doms, rows, cols = sizes
    dom, row, col = (lax.axis_index(name) for name in ("dom", "row", "col"))
    angles = currents.shape[1]
    width = currents.shape[2]
    window, tiles, rank, tile_len = self_v.shape[1:]
    links = coupling_u.shape[3]
    own_tiles = width // tile_len
    fold = max(1, LANES // rank)
    piece = angles // fold
    share = angles // cols

    def dom_at(k):
        return lax.rem(dom + k, doms)

    def row_at(k):
        return lax.rem(row + k, rows)

    def col_at(k):
        return lax.rem(col + k, cols)

    own_columns = pl.ds(pl.multiple_of(row * width, width), width)
    loads = [
        pltpu.make_async_copy(currents.at[0], cur_all.at[row], in_sem.at[0]),
        pltpu.make_async_copy(basis.at[0, :, own_columns], basis_own, in_sem.at[1]),
        pltpu.make_async_copy(self_v.at[0], v_buf, in_sem.at[2]),
        pltpu.make_async_copy(self_u.at[0], u_buf, in_sem.at[3]),
        pltpu.make_async_copy(coupling_u.at[0], cu_buf, in_sem.at[4]),
    ]
    for load in loads:
        load.start()

    barrier = pltpu.get_barrier_semaphore()
    for k in range(1, doms):
        pl.semaphore_signal(barrier, inc=1, device_id=(dom_at(k), row, col), device_id_type=MESH)
    for k in range(1, rows):
        pl.semaphore_signal(barrier, inc=1, device_id=(dom, row_at(k), col), device_id_type=MESH)
    for k in range(1, cols):
        pl.semaphore_signal(barrier, inc=1, device_id=(dom, row, col_at(k)), device_id_type=MESH)

    loads[0].wait()
    loads[1].wait()
    for o in range(own_tiles):
        span = slice(o * tile_len, (o + 1) * tile_len)
        own = lax.dot_general(
            cur_all[row, :, span], basis_own[:, span], NT, preferred_element_type=jnp.float32
        )
        folded = jnp.concatenate([own[f * piece : (f + 1) * piece] for f in range(fold)], axis=1)
        proj[dom, row, o] = folded.astype(jnp.bfloat16)

    pl.semaphore_wait(barrier, doms + rows + cols - 3)

    to_dom = [
        pltpu.make_async_remote_copy(
            src_ref=proj.at[dom, row],
            dst_ref=proj.at[dom, row],
            send_sem=dom_send.at[k - 1],
            recv_sem=dom_recv.at[k - 1],
            device_id=(dom_at(k), row, col),
            device_id_type=MESH,
        )
        for k in range(1, doms)
    ]
    for copy in to_dom:
        copy.start()

    def forward(source, slot):
        copies = [
            pltpu.make_async_remote_copy(
                src_ref=proj.at[source, row],
                dst_ref=proj.at[source, row],
                send_sem=row_send.at[slot, k - 1],
                recv_sem=row_recv.at[slot, k - 1],
                device_id=(dom, row_at(k), col),
                device_id_type=MESH,
            )
            for k in range(1, rows)
        ]
        for copy in copies:
            copy.start()
        return copies

    to_row = forward(dom, 0)
    spread = [
        pltpu.make_async_remote_copy(
            src_ref=cur_all.at[row],
            dst_ref=cur_all.at[row],
            send_sem=cur_send.at[k - 1],
            recv_sem=cur_recv.at[k - 1],
            device_id=(dom, row_at(k), col),
            device_id_type=MESH,
        )
        for k in range(1, rows)
    ]
    for copy in spread:
        copy.start()

    for k in range(1, doms):
        to_dom[k - 1].wait_recv()
        to_row += forward(dom_at(doms - k), k)

    lane = lax.broadcasted_iota(jnp.int32, (angles, rank), 1)
    for load in loads[2:]:
        load.wait()
    for copy in spread:
        copy.wait_recv()
    kept = [[] for _ in range(window)]
    for j in range(tiles):
        o = j % own_tiles
        cur = cur_all[j // own_tiles, :, o * tile_len : (o + 1) * tile_len]
        for t in range(window):
            level = lax.dot_general(cur, v_buf[t, j], NT, preferred_element_type=jnp.float32)
            kept[t].append(jnp.where(lane < self_rank[0, t, j], level, 0.0))
    for t in range(window):
        left = jnp.concatenate(kept[t], axis=1).astype(jnp.bfloat16)
        acc[t] = jnp.dot(
            left, u_buf[t].reshape(tiles * rank, tile_len), preferred_element_type=jnp.float32
        )

    for copy in to_row:
        copy.wait_recv()
    pick_lane = lax.broadcasted_iota(jnp.int32, (piece, rank), 1)
    to_col = []
    for t in range(window):
        lefts = [[] for _ in range(fold)]
        for e in range(doms):
            for m in range(links):
                tile = link_tiles[0, t, m, e]
                held = proj[e, tile // own_tiles, tile % own_tiles] if own_tiles > 1 else proj[e, tile, 0]
                held = held.astype(jnp.float32)
                keep = pick_lane < coupling_rank[0, t, m, e]
                for f in range(fold):
                    lefts[f].append(jnp.where(keep, held[:, f * rank : (f + 1) * rank], 0.0))
        left = jnp.concatenate([jnp.concatenate(one, axis=1) for one in lefts], axis=0)
        part[t] = acc[t] + jnp.dot(
            left.astype(jnp.bfloat16),
            cu_buf[t].reshape(doms * links * rank, tile_len),
            preferred_element_type=jnp.float32,
        )
        for k in range(1, cols):
            theirs = pl.ds(pl.multiple_of(col_at(k) * share, share), share)
            copy = pltpu.make_async_remote_copy(
                src_ref=part.at[t, theirs],
                dst_ref=landed.at[k - 1, t],
                send_sem=col_send.at[k - 1, t],
                recv_sem=col_recv.at[k - 1, t],
                device_id=(dom, row, col_at(k)),
                device_id_type=MESH,
            )
            copy.start()
            to_col.append(copy)

    for copy in to_dom + to_row + spread:
        copy.wait_send()
    mine = pl.ds(pl.multiple_of(col * share, share), share)
    for t in range(window):
        total = part[t, mine]
        for k in range(1, cols):
            to_col[t * (cols - 1) + k - 1].wait_recv()
            total = total + landed[k - 1, t]
        out[:, t * tile_len : (t + 1) * tile_len] = total
    for copy in to_col:
        copy.wait_send()


def shards(
    currents,
    shared_basis,
    self_v,
    self_u,
    self_rank,
    coupling_u,
    coupling_rank,
    link_tiles,
    incident,
):
    doms, rows, cols = (lax.axis_size(name) for name in ("dom", "row", "col"))
    angles, width = currents.shape[1:]
    window, tiles, rank, tile_len = self_v.shape[1:]
    links = coupling_u.shape[3]
    own_tiles = width // tile_len
    fold = max(1, LANES // rank)
    share = angles // cols
    bf16, f32 = jnp.bfloat16, jnp.float32
    dma = pltpu.SemaphoreType.DMA
    smem = pl.BlockSpec(memory_space=pltpu.SMEM)
    stay = pl.BlockSpec(memory_space=pl.ANY)
    summed = pl.pallas_call(
        functools.partial(kernel, (doms, rows, cols)),
        out_shape=jax.ShapeDtypeStruct((share, window * tile_len), f32),
        in_specs=[smem] * 3 + [stay] * 5,
        out_specs=pl.BlockSpec(memory_space=pltpu.VMEM),
        scratch_shapes=[
            pltpu.VMEM((rows, angles, width), bf16),
            pltpu.VMEM((rank, width), bf16),
            pltpu.VMEM((window, tiles, rank, tile_len), bf16),
            pltpu.VMEM((window, tiles, rank, tile_len), bf16),
            pltpu.VMEM((window, doms, links, rank, tile_len), bf16),
            pltpu.VMEM((doms, rows, own_tiles, angles // fold, fold * rank), bf16),
            pltpu.VMEM((window, angles, tile_len), f32),
            pltpu.VMEM((window, angles, tile_len), f32),
            pltpu.VMEM((cols - 1, window, share, tile_len), f32),
            dma((5,)),
            dma((rows - 1,)),
            dma((rows - 1,)),
            dma((doms - 1,)),
            dma((doms - 1,)),
            dma((doms, rows - 1)),
            dma((doms, rows - 1)),
            dma((cols - 1, window)),
            dma((cols - 1, window)),
        ],
        compiler_params=pltpu.CompilerParams(collective_id=0, has_side_effects=True),
    )(self_rank, jnp.swapaxes(coupling_rank, 2, 3), jnp.swapaxes(link_tiles, 2, 3), currents, shared_basis, self_v, self_u, coupling_u)
    return (incident[0] - summed)[None]


def solution(mesh):
    return jax.shard_map(
        shards,
        mesh=mesh,
        in_specs=(
            P("dom", None, ("col", "row")),
            P("dom", None, "col"),
            P("dom", "row", "col", None, None),
            P("dom", "row", "col", None, None),
            P("dom", "row", "col"),
            P("dom", "row", None, "col", None, None),
            P("dom", "row", None, "col"),
            P("dom", "row", None, "col"),
            P("dom", "col", "row"),
        ),
        out_specs=P("dom", "col", "row"),
        check_vma=False,
    )
```

time: 54.9 us -> 17.4 us (0.32)
  blocking collectives: 25.3 us -> 0 us
  Pallas kernels: 0 us -> 15.7 us
  between operations: 13.5 us -> 0.02 us
  waiting for transfers between devices: 7.66 us -> 0 us
  local copies, waits for them, and re-layouts: 5.2 us -> 0.01 us
  matrix products: 1.23 us -> 0 us
    all_gather x2 -> x0, blocking collectives: 25.3 us -> none  [the longest x1 14.4 us: shards(): flat_proj = lax.all_gather(projections, 'dom', axis=0, tiled=True)]
    pallas_call x0 -> x1, Pallas kernels: none -> 15.7 us  [shards(): pl.pallas_call(functools.partial(kernel, (doms, rows, cols)), out_shape=j...]
    reduce_scatter x1 -> x0, waiting for transfers between devices: 7.64 us -> none  [shards(): lax.psum_scatter((field_self + field_cpl).reshape(lax.axis_size('col') *...]
    unnamed x17 -> x2, local copies, waits for them, and re-layouts: 2.88 us -> 0.01 us
    dot_general x3 -> x0, matrix products: 1.23 us -> none  [the longest x1 0.6 us: shards(): jnp.einsum('tjkn,tjka->atn', self_u[0], selfproj, preferred_element_type=...]
    gather x2 -> x0, local copies, waits for them, and re-layouts: 0.78 us -> none  [shards(): chosen = jnp.take(flat_proj, picks.reshape(-1), axis=0)]
    reshape x1 -> x0, local copies, waits for them, and re-layouts: 0.71 us -> none  [shards(): (field_self + field_cpl).reshape(lax.axis_size('col') * (angles // col_co...]
  transfers between devices with their start and end apart: 1 -> 0, of which waited for: 1 -> 0; matrix products, arithmetic and copies ran while one was open for 0% -> 0% of each run, Pallas kernels for 0% -> 0%
where the time goes in v1:
time: 17.4 us; the launch traced here: 17.2 us
  Pallas kernels  15.7 us (90%)
  other arithmetic  1.58 us (9%)
    pallas_call x1, Pallas kernels, shards(): pl.pallas_call(functools.partial(kernel, (doms, rows, cols)), out_shape=j...  15.7 us
    broadcast_in_dim x1, other arithmetic, shards(): return (incident[0] - summed)[None]  1.58 us

profile of v1, /device:TPU:0, one launch (start us, length us, event | category | flops | bytes accessed | tf_op | source)
XLA Modules:
  0.0 17.2 jit_solution(12077468665306033984)
XLA Ops:
  0.0 0.0 copy-start
  0.0 15.7 %shard_map.91 = f32[32,1024]{1,0:T(8,128)} custom-call(s32[1,2,4]{2,1,0:T(2,128)} %self_rank.1, s32[1,2,2,4]{3,2,1,0:T(2,128)} %bitcast.8, s32[1,2,2,4]{3,2,1,0:T(2,128)} %bitcast.9, bf16[1,64,512]{2,1,0:T(8,128)(2,1)} %currents.1, bf16[1,64,2048]{2,1,0:T(8,128)(2,1)} %basis.1, bf16[1,2,4,64,512]{4,3,2,1,0:T(8,128)(2,1)} %self_v.1, ...), custom_call_target="tpu_custom_call" | custom-call | tf_op jit(solution)/shard_map/pallas_call | solution.py:231
  15.7 0.0 copy-done
  15.7 1.6 %fusion = f32[1,32,1024]{2,1,0:T(8,128)} fusion(f32[32,1024]{1,0:T(8,128)} %shard_map.91, f32[1,32,1024]{2,1,0:T(8,128)S(1)} %copy-done), kind=kLoop, calls=%fused_computation.1 | loop fusion | flops 32768 | bytes 393216 | tf_op jit(solution)/shard_map/broadcast_in_dim | solution.py:258
Async XLA Ops:
  0.0 15.7 %copy-start = (f32[1,32,1024]{2,1,0:T(8,128)S(1)}, f32[1,32,1024]{2,1,0:T(8,128)}, u32[]{:S(2)}) copy-start(f32[1,32,1024]{2,1,0:T(8,128)} %param.17) | copy-start | bytes 393220

commit v2 on v1

--- a/solution.py
+++ b/solution.py
@@ -14,15 +14,18 @@
 
 def kernel(
     sizes,
-    self_rank,
-    coupling_rank,
-    link_tiles,
+    self_rank_in,
+    coupling_rank_in,
+    link_tiles_in,
     currents,
     basis,
     self_v,
     self_u,
     coupling_u,
     out,
+    self_rank,
+    coupling_rank,
+    link_tiles,
     cur_all,
     basis_own,
     v_buf,
@@ -69,6 +72,9 @@
         pltpu.make_async_copy(self_v.at[0], v_buf, in_sem.at[2]),
         pltpu.make_async_copy(self_u.at[0], u_buf, in_sem.at[3]),
         pltpu.make_async_copy(coupling_u.at[0], cu_buf, in_sem.at[4]),
+        pltpu.make_async_copy(self_rank_in, self_rank, in_sem.at[5]),
+        pltpu.make_async_copy(coupling_rank_in, coupling_rank, in_sem.at[6]),
+        pltpu.make_async_copy(link_tiles_in, link_tiles, in_sem.at[7]),
     ]
     for load in loads:
         load.start()
@@ -226,14 +232,17 @@
     share = angles // cols
     bf16, f32 = jnp.bfloat16, jnp.float32
     dma = pltpu.SemaphoreType.DMA
-    smem = pl.BlockSpec(memory_space=pltpu.SMEM)
-    stay = pl.BlockSpec(memory_space=pl.ANY)
+    stay = pl.BlockSpec(memory_space=pltpu.HBM)
+    ranks, picks = (jnp.swapaxes(x, 2, 3) for x in (coupling_rank, link_tiles))
     summed = pl.pallas_call(
         functools.partial(kernel, (doms, rows, cols)),
         out_shape=jax.ShapeDtypeStruct((share, window * tile_len), f32),
-        in_specs=[smem] * 3 + [stay] * 5,
+        in_specs=[stay] * 8,
         out_specs=pl.BlockSpec(memory_space=pltpu.VMEM),
         scratch_shapes=[
+            pltpu.SMEM(self_rank.shape, jnp.int32),
+            pltpu.SMEM(ranks.shape, jnp.int32),
+            pltpu.SMEM(picks.shape, jnp.int32),
             pltpu.VMEM((rows, angles, width), bf16),
             pltpu.VMEM((rank, width), bf16),
             pltpu.VMEM((window, tiles, rank, tile_len), bf16),
@@ -243,7 +252,7 @@
             pltpu.VMEM((window, angles, tile_len), f32),
             pltpu.VMEM((window, angles, tile_len), f32),
             pltpu.VMEM((cols - 1, window, share, tile_len), f32),
-            dma((5,)),
+            dma((8,)),
             dma((rows - 1,)),
             dma((rows - 1,)),
             dma((doms - 1,)),
@@ -253,8 +262,8 @@
             dma((cols - 1, window)),
             dma((cols - 1, window)),
         ],
-        compiler_params=pltpu.CompilerParams(collective_id=0, has_side_effects=True),
-    )(self_rank, jnp.swapaxes(coupling_rank, 2, 3), jnp.swapaxes(link_tiles, 2, 3), currents, shared_basis, self_v, self_u, coupling_u)
+        compiler_params=pltpu.CompilerParams(collective_id=0, has_side_effects=True, vmem_limit_bytes=16 << 20),
+    )(*(pltpu.with_memory_space_constraint(x, pltpu.HBM) for x in (self_rank, ranks, picks, currents, shared_basis, self_v, self_u, coupling_u)))
     return (incident[0] - summed)[None]
 
 

time: 17.4 us -> 15 us (0.86)
  Pallas kernels: 15.7 us -> 14.2 us
  other arithmetic: 1.58 us -> 0.67 us
    pallas_call x1, Pallas kernels: 15.7 us -> 14.2 us  [shards(): pl.pallas_call(functools.partial(kernel, (doms, rows, cols)), out_shape=j...]
    broadcast_in_dim x1, other arithmetic: 1.58 us -> 0.67 us  [shards(): return (incident[0] - summed)[None]]
where the time goes in v2:
time: 15 us; the launch traced here: 14.9 us
  Pallas kernels  14.2 us (95%)
  other arithmetic  0.67 us (4%)
    pallas_call x1, Pallas kernels, shards(): pl.pallas_call(functools.partial(kernel, (doms, rows, cols)), out_shape=j...  14.2 us
    broadcast_in_dim x1, other arithmetic, shards(): return (incident[0] - summed)[None]  0.67 us

profile of v2, /device:TPU:0, one launch (start us, length us, event | category | flops | bytes accessed | tf_op | source)
XLA Modules:
  0.0 14.9 jit_solution(18272898370418595299)
XLA Ops:
  0.0 0.0 copy-start
  0.0 14.2 %shard_map.91 = f32[32,1024]{1,0:T(8,128)S(1)} custom-call(s32[1,2,4]{2,1,0:T(2,128)} %self_rank_in.1, s32[1,2,2,4]{3,2,1,0:T(2,128)} %bitcast.8, s32[1,2,2,4]{3,2,1,0:T(2,128)} %bitcast.9, bf16[1,64,512]{2,1,0:T(8,128)(2,1)} %currents.1, bf16[1,64,2048]{2,1,0:T(8,128)(2,1)} %basis.1, bf16[1,2,4,64,512]{4,3,2,1,0:T(8,128)(2,1)} %self_v.1, ...), custom_call_target="tpu_custom_call" | custom-call | tf_op jit(solution)/shard_map/pallas_call | solution.py:237
  14.2 0.0 copy-done
  14.2 0.7 %fusion = f32[1,32,1024]{2,1,0:T(8,128)} fusion(f32[32,1024]{1,0:T(8,128)S(1)} %shard_map.91, f32[1,32,1024]{2,1,0:T(8,128)S(1)} %copy-done), kind=kLoop, calls=%fused_computation.1 | loop fusion | flops 32768 | bytes 393216 | tf_op jit(solution)/shard_map/broadcast_in_dim | solution.py:267
Async XLA Ops:
  0.0 14.2 %copy-start = (f32[1,32,1024]{2,1,0:T(8,128)S(1)}, f32[1,32,1024]{2,1,0:T(8,128)}, u32[]{:S(2)}) copy-start(f32[1,32,1024]{2,1,0:T(8,128)} %param.17) | copy-start | bytes 393220

commit v3 on v2

--- a/solution.py
+++ b/solution.py
@@ -44,6 +44,9 @@
     row_recv,
     col_send,
     col_recv,
+    straight_send,
+    above,
+    *hold,
 ):
     doms, rows, cols = sizes
     dom, row, col = (lax.axis_index(name) for name in ("dom", "row", "col"))
@@ -81,13 +84,38 @@
 
     barrier = pltpu.get_barrier_semaphore()
     for k in range(1, doms):
-        pl.semaphore_signal(barrier, inc=1, device_id=(dom_at(k), row, col), device_id_type=MESH)
+
+        @pl.when(dom + k < doms)
+        def _():
+            for b in range(rows):
+                pl.semaphore_signal(barrier, inc=1, device_id=(dom_at(k), row_at(b), col), device_id_type=MESH)
+
     for k in range(1, rows):
         pl.semaphore_signal(barrier, inc=1, device_id=(dom, row_at(k), col), device_id_type=MESH)
     for k in range(1, cols):
         pl.semaphore_signal(barrier, inc=1, device_id=(dom, row, col_at(k)), device_id_type=MESH)
+    pl.semaphore_wait(barrier, dom * rows + rows + cols - 2)
+    for k in range(1, doms):
+
+        @pl.when(dom + k >= doms)
+        def _():
+            pl.semaphore_signal(above, inc=1, device_id=(dom_at(k), row, col), device_id_type=MESH)
 
     loads[0].wait()
+    spread = [
+        pltpu.make_async_remote_copy(
+            src_ref=cur_all.at[row],
+            dst_ref=cur_all.at[row],
+            send_sem=cur_send.at[k - 1],
+            recv_sem=cur_recv.at[k - 1],
+            device_id=(dom, row_at(k), col),
+            device_id_type=MESH,
+        )
+        for k in range(1, rows)
+    ]
+    for copy in spread:
+        copy.start()
+
     loads[1].wait()
     for o in range(own_tiles):
         span = slice(o * tile_len, (o + 1) * tile_len)
@@ -97,21 +125,38 @@
         folded = jnp.concatenate([own[f * piece : (f + 1) * piece] for f in range(fold)], axis=1)
         proj[dom, row, o] = folded.astype(jnp.bfloat16)
 
-    pl.semaphore_wait(barrier, doms + rows + cols - 3)
-
     to_dom = [
         pltpu.make_async_remote_copy(
             src_ref=proj.at[dom, row],
             dst_ref=proj.at[dom, row],
-            send_sem=dom_send.at[k - 1],
-            recv_sem=dom_recv.at[k - 1],
+            send_sem=dom_send.at[k],
+            recv_sem=dom_recv.at[k],
             device_id=(dom_at(k), row, col),
             device_id_type=MESH,
         )
         for k in range(1, doms)
     ]
-    for copy in to_dom:
-        copy.start()
+    straight = [
+        [
+            pltpu.make_async_remote_copy(
+                src_ref=proj.at[dom, row],
+                dst_ref=proj.at[dom, row],
+                send_sem=straight_send.at[k, b - 1],
+                recv_sem=row_recv.at[k, b - 1],
+                device_id=(dom_at(k), row_at(b), col),
+                device_id_type=MESH,
+            )
+            for b in range(1, rows)
+        ]
+        for k in range(1, doms)
+    ]
+    for k in range(1, doms):
+
+        @pl.when(dom + k >= doms)
+        def _():
+            to_dom[k - 1].start()
+            for copy in straight[k - 1]:
+                copy.start()
 
     def forward(source, slot):
         copies = [
@@ -125,28 +170,39 @@
             )
             for k in range(1, rows)
         ]
-        for copy in copies:
-            copy.start()
+
+        @pl.when(slot <= dom)
+        def _():
+            for copy in copies:
+                copy.start()
+
         return copies
 
-    to_row = forward(dom, 0)
-    spread = [
+    to_row = [forward(dom, 0)]
+
+    @pl.when(dom + 1 < doms)
+    def _():
+        pl.semaphore_wait(above, doms - 1 - dom)
+
+    for k in range(1, doms):
+
+        @pl.when(dom + k < doms)
+        def _():
+            to_dom[k - 1].start()
+
+    lower = 1 - (2 * dom) // doms
+    steps = [0] + [i + (doms - 2 * i) * lower for i in range(1, doms)]
+    sources = [dom] + [dom_at(doms - k) for k in steps[1:]]
+    for k, source in zip(steps[1:], sources[1:]):
         pltpu.make_async_remote_copy(
-            src_ref=cur_all.at[row],
-            dst_ref=cur_all.at[row],
-            send_sem=cur_send.at[k - 1],
-            recv_sem=cur_recv.at[k - 1],
-            device_id=(dom, row_at(k), col),
+            src_ref=proj.at[source, row],
+            dst_ref=proj.at[source, row],
+            send_sem=dom_send.at[k],
+            recv_sem=dom_recv.at[k],
+            device_id=(source, row, col),
             device_id_type=MESH,
-        )
-        for k in range(1, rows)
-    ]
-    for copy in spread:
-        copy.start()
-
-    for k in range(1, doms):
-        to_dom[k - 1].wait_recv()
-        to_row += forward(dom_at(doms - k), k)
+        ).wait_recv()
+        to_row.append(forward(source, k))
 
     lane = lax.broadcasted_iota(jnp.int32, (angles, rank), 1)
     for load in loads[2:]:
@@ -166,41 +222,66 @@
             left, u_buf[t].reshape(tiles * rank, tile_len), preferred_element_type=jnp.float32
         )
 
-    for copy in to_row:
-        copy.wait_recv()
     pick_lane = lax.broadcasted_iota(jnp.int32, (piece, rank), 1)
+
+    def coupled(t, e, held_all):
+        lefts = [[] for _ in range(fold)]
+        for m in range(links):
+            tile = link_tiles[0, t, m, e]
+            held = held_all[tile].astype(jnp.float32)
+            keep = pick_lane < coupling_rank[0, t, m, e]
+            for f in range(fold):
+                lefts[f].append(jnp.where(keep, held[:, f * rank : (f + 1) * rank], 0.0))
+        left = jnp.concatenate([jnp.concatenate(one, axis=1) for one in lefts], axis=0)
+        return jnp.dot(
+            left.astype(jnp.bfloat16),
+            cu_buf[t, e].reshape(links * rank, tile_len),
+            preferred_element_type=jnp.float32,
+        )
+
     to_col = []
-    for t in range(window):
-        lefts = [[] for _ in range(fold)]
-        for e in range(doms):
-            for m in range(links):
-                tile = link_tiles[0, t, m, e]
-                held = proj[e, tile // own_tiles, tile % own_tiles] if own_tiles > 1 else proj[e, tile, 0]
-                held = held.astype(jnp.float32)
-                keep = pick_lane < coupling_rank[0, t, m, e]
-                for f in range(fold):
-                    lefts[f].append(jnp.where(keep, held[:, f * rank : (f + 1) * rank], 0.0))
-        left = jnp.concatenate([jnp.concatenate(one, axis=1) for one in lefts], axis=0)
-        part[t] = acc[t] + jnp.dot(
-            left.astype(jnp.bfloat16),
-            cu_buf[t].reshape(doms * links * rank, tile_len),
-            preferred_element_type=jnp.float32,
-        )
-        for k in range(1, cols):
-            theirs = pl.ds(pl.multiple_of(col_at(k) * share, share), share)
-            copy = pltpu.make_async_remote_copy(
-                src_ref=part.at[t, theirs],
-                dst_ref=landed.at[k - 1, t],
-                send_sem=col_send.at[k - 1, t],
-                recv_sem=col_recv.at[k - 1, t],
-                device_id=(dom, row, col_at(k)),
-                device_id_type=MESH,
-            )
-            copy.start()
-            to_col.append(copy)
-
-    for copy in to_dom + to_row + spread:
+    for i, e in enumerate(sources):
+        for copy in to_row[i]:
+            copy.wait_recv()
+        held_all = hold[i]
+        for r in range(rows):
+            for o in range(own_tiles):
+                held_all[r * own_tiles + o] = proj[e, r, o]
+        if i < doms - 1:
+            for t in range(window):
+                acc[t] += coupled(t, e, held_all)
+            continue
+        for t in range(window):
+            part[t] = acc[t] + coupled(t, e, held_all)
+            for k in range(1, cols):
+                theirs = pl.ds(pl.multiple_of(col_at(k) * share, share), share)
+                copy = pltpu.make_async_remote_copy(
+                    src_ref=part.at[t, theirs],
+                    dst_ref=landed.at[k - 1, t],
+                    send_sem=col_send.at[k - 1, t],
+                    recv_sem=col_recv.at[k - 1, t],
+                    device_id=(dom, row, col_at(k)),
+                    device_id_type=MESH,
+                )
+                copy.start()
+                to_col.append(copy)
+
+    for copy in to_dom + to_row[0] + spread:
         copy.wait_send()
+    for k in range(1, doms):
+
+        @pl.when(dom + k >= doms)
+        def _():
+            for copy in straight[k - 1]:
+                copy.wait_send()
+
+    for k, copies in zip(steps[1:], to_row[1:]):
+
+        @pl.when(k <= dom)
+        def _():
+            for copy in copies:
+                copy.wait_send()
+
     mine = pl.ds(pl.multiple_of(col * share, share), share)
     for t in range(window):
         total = part[t, mine]
@@ -255,13 +336,16 @@
             dma((8,)),
             dma((rows - 1,)),
             dma((rows - 1,)),
-            dma((doms - 1,)),
-            dma((doms - 1,)),
+            dma((doms,)),
+            dma((doms,)),
             dma((doms, rows - 1)),
             dma((doms, rows - 1)),
             dma((cols - 1, window)),
             dma((cols - 1, window)),
-        ],
+            dma((doms, rows - 1)),
+            pltpu.SemaphoreType.REGULAR,
+        ]
+        + [pltpu.VMEM((rows * own_tiles, angles // fold, fold * rank), bf16)] * doms,
         compiler_params=pltpu.CompilerParams(collective_id=0, has_side_effects=True, vmem_limit_bytes=16 << 20),
     )(*(pltpu.with_memory_space_constraint(x, pltpu.HBM) for x in (self_rank, ranks, picks, currents, shared_basis, self_v, self_u, coupling_u)))
     return (incident[0] - summed)[None]

time: 15 us -> 14 us (0.933)
  the two profiles are of different devices: /device:TPU:0 before, /device:TPU:17 now
where the time goes in v3:
time: 14 us; the launch traced here: 13.8 us
  Pallas kernels  13.1 us (94%)
  other arithmetic  0.67 us (5%)
    pallas_call x1, Pallas kernels, shards(): pl.pallas_call(functools.partial(kernel, (doms, rows, cols)), out_shape=j...  13.1 us
    broadcast_in_dim x1, other arithmetic, shards(): return (incident[0] - summed)[None]  0.67 us

profile of v3, /device:TPU:17, one launch (start us, length us, event | category | flops | bytes accessed | tf_op | source)
XLA Modules:
  0.0 13.8 jit_solution(18306032310385686225)
XLA Ops:
  0.0 0.0 copy-start
  0.0 13.1 %shard_map.91 = f32[32,1024]{1,0:T(8,128)S(1)} custom-call(s32[1,2,4]{2,1,0:T(2,128)} %self_rank_in.1, s32[1,2,2,4]{3,2,1,0:T(2,128)} %bitcast.8, s32[1,2,2,4]{3,2,1,0:T(2,128)} %bitcast.9, bf16[1,64,512]{2,1,0:T(8,128)(2,1)} %currents.1, bf16[1,64,2048]{2,1,0:T(8,128)(2,1)} %basis.1, bf16[1,2,4,64,512]{4,3,2,1,0:T(8,128)(2,1)} %self_v.1, ...), custom_call_target="tpu_custom_call" | custom-call | tf_op jit(solution)/shard_map/pallas_call | solution.py:318
  13.1 0.0 copy-done
  13.1 0.7 %fusion = f32[1,32,1024]{2,1,0:T(8,128)} fusion(f32[32,1024]{1,0:T(8,128)S(1)} %shard_map.91, f32[1,32,1024]{2,1,0:T(8,128)S(1)} %copy-done), kind=kLoop, calls=%fused_computation.1 | loop fusion | flops 32768 | bytes 393216 | tf_op jit(solution)/shard_map/broadcast_in_dim | solution.py:351
Async XLA Ops:
  0.0 13.1 %copy-start = (f32[1,32,1024]{2,1,0:T(8,128)S(1)}, f32[1,32,1024]{2,1,0:T(8,128)}, u32[]{:S(2)}) copy-start(f32[1,32,1024]{2,1,0:T(8,128)} %param.17) | copy-start | bytes 393220
